TPU v7x, 32 devices: a whole 2x2x4 slice. The times are simulated.
32 devices in a mesh: group: 2 (over x), dp: 2 (over core), tensor: 8 (over z, y).
Axes of the slice: x: 2, y: 2, z: 4, core: 2. Of those that a mesh axis runs over, the one named last changes fastest.
Arguments:
- teacher_hidden: bfloat16 [1024, 8192], P(('group', 'dp'), 'tensor'), may hold values from -6 to 6
- teacher_gain: float32 [8192], P('tensor'), may hold values from 0.1 to 1.9
- project_weight: bfloat16 [8192, 3584], P('tensor'), may hold values from -0.0625 to 0.0625
- student_hidden: bfloat16 [1024, 3584], P(('group', 'dp', 'tensor')), may hold values from -6 to 6
- student_gain: float32 [3584], replicated, may hold values from 0.1 to 1.9
- gate_weight: bfloat16 [3584, 9472], P(('group', 'dp'), 'tensor'), may hold values from -0.09375 to 0.09375
- up_weight: bfloat16 [3584, 9472], P(('group', 'dp'), 'tensor'), may hold values from -0.09375 to 0.09375
- down_weight: bfloat16 [9472, 3584], P('tensor', ('group', 'dp')), may hold values from -0.0625 to 0.0625
- owner_map: int32 [64, 1], P(('group', 'dp')), may hold values from 0 to 3; in each aligned block of 16 rows (0 to 15, 16 to 31, ...) at most 8 rows name the same one
- token_ids: int32 [1024], P(('group', 'dp', 'tensor')), may hold values from 0 to 511
- token_counts: int32 [64], P(('group', 'dp')), may hold values from 1 to 16
- id_weight: float32 [512], replicated, may hold values from 0.25 to 4
Outputs:
- student_out: bfloat16 [4, 16, 32, 3584], P(('group', 'dp'), 'tensor')
- down_grad: float32 [3584, 9472], P(('group', 'dp'), 'tensor')
Inputs may be any that keep to these rules, and one draw needn't show every extreme that they name: `owner_map`: of the 16 episodes of one index of group and dp (aligned blocks of 16 rows), at most 8 have the same owner; owner o is index o of group and dp in mesh order.
All inputs are finite; a program needn't handle non-finite values.
Results may differ from a plain program's by a relative error of at most 0.02.
Values may be sent and summed in bfloat16 or wider, within the bound.
A program may use at most 128 MiB of HBM per device.

v0:
```python
import math

import jax
import jax.numpy as jnp
from jax import lax
from jax.sharding import PartitionSpec as P

DT = 8192
EP_LEN = 16


EPSILON = 1e-06


def build_selector(owner_local, owners, capacity):
    owner_list = owner_local[:, 0]
    onehot = (owner_list[:, None] == jnp.arange(owners, dtype=jnp.int32)[None, :]).astype(jnp.int32)
    earlier = jnp.cumsum(onehot, axis=0) - onehot
    rank_list = jnp.sum(earlier * onehot, axis=1)
    target = owner_list * capacity + rank_list
    return (target[None, :] == jnp.arange(owners * capacity, dtype=jnp.int32)[:, None]).astype(
        jnp.bfloat16
    )


def dispatch_rows(selector, values):
    return jnp.einsum("re,pef->prf", selector, values, preferred_element_type=jnp.float32).astype(
        jnp.bfloat16
    )


def dispatch_plain(selector, values):
    return jnp.einsum("re,pe->pr", selector, values, preferred_element_type=jnp.float32).astype(
        jnp.bfloat16
    )


def regroup_rows(payload):
    return (
        lax.all_to_all(payload[0], ("group", "dp"), split_axis=1, concat_axis=1, tiled=True),
        lax.all_to_all(payload[1], ("group", "dp"), split_axis=1, concat_axis=1, tiled=True),
        lax.all_to_all(payload[2], ("group", "dp"), split_axis=1, concat_axis=1, tiled=True),
    )


def teacher_scaling(raw_rows, teacher_gain):
    widened = raw_rows.astype(jnp.float32)
    return (
        jnp.sum(widened * widened, axis=1),
        (widened * teacher_gain[None, :]).astype(jnp.bfloat16),
    )


def local(
    teacher_hidden,
    teacher_gain,
    project_weight,
    student_hidden,
    student_gain,
    gate_weight,
    up_weight,
    down_weight,
    owner_map,
    token_ids,
    token_counts,
    id_weight,
):
    groups = lax.axis_size("group")
    places = lax.axis_size("dp")
    owners = groups * places
    tensors = lax.axis_size("tensor")
    tensor_index = lax.axis_index("tensor")
    episodes = token_counts.shape[0]
    own_span = EP_LEN // tensors
    capacity = max(2, 2 * episodes // owners)
    received = owners * capacity
    student_width = student_hidden.shape[1]
    selector = build_selector(owner_map, owners, capacity)
    id_rows = token_ids.reshape(own_span, episodes)
    looked = jnp.sum(
        jnp.where(
            id_rows[:, :, None] == jnp.arange(id_weight.shape[0], dtype=jnp.int32)[None, None, :],
            id_weight[None, None, :],
            0.0,
        ),
        axis=2,
    )
    position = tensor_index * own_span + jnp.arange(own_span, dtype=jnp.int32)[:, None]
    token_weight = jnp.where(position < token_counts[None, :], looked, 0.0).astype(jnp.bfloat16)
    sent_weight = dispatch_plain(selector, token_weight)
    sent_student = dispatch_rows(
        selector, student_hidden.reshape(own_span, episodes, student_width)
    )
    squares, scaled = teacher_scaling(teacher_hidden, teacher_gain)
    totals = lax.psum(squares, "tensor")
    inverse = lax.rsqrt(totals / DT + EPSILON)
    share_rows = own_span * episodes
    summed = lax.psum_scatter(
        jnp.dot(scaled, project_weight, preferred_element_type=jnp.float32).astype(jnp.bfloat16),
        "tensor",
        scatter_dimension=0,
        tiled=True,
    ).astype(jnp.float32)
    own_inverse = lax.dynamic_slice_in_dim(inverse, tensor_index * share_rows, share_rows, 0)
    projected = (
        (summed * own_inverse[:, None])
        .astype(jnp.bfloat16)
        .reshape(own_span, episodes, student_width)
    )
    arrived = regroup_rows((dispatch_rows(selector, projected), sent_student, sent_weight))
    teacher_mine = arrived[0]
    student_block = arrived[1].reshape(own_span * received, student_width).astype(jnp.float32)
    rescale = lax.rsqrt(jnp.mean(student_block * student_block, axis=1, keepdims=True) + EPSILON)
    normed = (student_block * rescale * student_gain[None, :]).astype(jnp.bfloat16)
    gathered = lax.all_gather(normed, "tensor", axis=0, tiled=True)
    gate_sum = jnp.dot(
        gathered,
        lax.all_gather(gate_weight, ("group", "dp"), axis=0, tiled=True),
        preferred_element_type=jnp.float32,
    )
    up_sum = jnp.dot(
        gathered,
        lax.all_gather(up_weight, ("group", "dp"), axis=0, tiled=True),
        preferred_element_type=jnp.float32,
    )
    activated = (jax.nn.silu(gate_sum) * up_sum).astype(jnp.bfloat16)
    branch = jnp.dot(
        activated,
        lax.all_gather(down_weight, ("group", "dp"), axis=1, tiled=True),
        preferred_element_type=jnp.float32,
    )
    branch_local = lax.psum_scatter(
        branch.astype(jnp.bfloat16), "tensor", scatter_dimension=0, tiled=True
    ).astype(jnp.float32)
    predicted = student_block + branch_local
    student_out = predicted.astype(jnp.bfloat16).reshape(1, own_span, received, student_width)
    difference = predicted - teacher_mine.reshape(-1, student_width).astype(jnp.float32)
    weight_rows = arrived[2].reshape(-1, 1).astype(jnp.float32)
    tokens_all = EP_LEN * episodes * owners
    grad_block = (weight_rows * difference * (1.0 / math.sqrt(tokens_all))).astype(jnp.bfloat16)
    grad_all = lax.all_gather(grad_block, "tensor", axis=0, tiled=True)
    down_grad = lax.psum_scatter(
        jnp.einsum("rc,rh->ch", grad_all, activated, preferred_element_type=jnp.float32).astype(
            jnp.bfloat16
        ),
        ("group", "dp"),
        scatter_dimension=0,
        tiled=True,
    ).astype(jnp.float32)
    return (student_out, down_grad)


def solution(mesh):
    in_specs = (
        P(("group", "dp"), "tensor"),
        P("tensor"),
        P("tensor", None),
        P(("group", "dp", "tensor"), None),
        P(),
        P(("group", "dp"), "tensor"),
        P(("group", "dp"), "tensor"),
        P("tensor", ("group", "dp")),
        P(("group", "dp"), None),
        P(("group", "dp", "tensor")),
        P(("group", "dp")),
        P(),
    )
    out_specs = (P(("group", "dp"), "tensor", None, None), P(("group", "dp"), "tensor"))
    return jax.shard_map(local, mesh=mesh, in_specs=in_specs, out_specs=out_specs, check_vma=False)
```

profile of v0, /device:TPU:0, one launch (start us, length us, event | category | flops | bytes accessed | tf_op | source)
XLA Modules:
  0.0 602.6 jit_solution(13602715377556277750)
XLA Ops:
  7.2 0.8 fusion.17
  8.0 0.8 select_reduce_fusion.1
  8.9 0.7 multiply_add_fusion
  10.4 12.1 %all_to_all.19 = bf16[2,32,3584]{2,0,1:T(2,128)(2,1)S(1)} all-to-all(bf16[2,32,3584]{2,0,1:T(2,128)(2,1)S(1)} %copy.34), channel_id=1, replica_groups=mesh['group'=2,'dp'=2,'tensor'=8] {'group','dp'}, dimensions={1} | all-to-all | bytes 917504 | tf_op jit(solution)/shard_map/all_to_all | solution.py:41
  22.8 1.7 fusion.10
  24.6 0.7 all-gather.8.cloned.1.call-update
  25.4 0.7 all-gather.10.cloned.1.call-update
  26.7 6.4 %convolution_convert_fusion.2 = bf16[256,3584]{1,0:T(8,128)(2,1)} fusion(bf16[1024,3584]{1,0:T(8,128)(2,1)} %param.14, bf16[256,1024]{1,0:T(8,128)(2,1)S(1)} %copy-done.2, f32[1024]{0:T(1024)S(1)} %copy-done.4), kind=kOutput, calls=%fused_computation.2 | convolution fusion | flops 1880752128 | bytes 9703424 | tf_op jit(solution)/shard_map/dot_general | solution.py:99
  33.2 58.1 %all-gather.6.cloned.1.call-done = bf16[512,3584]{1,0:T(8,128)(2,1)} async-done(((bf16[64,3584]{1,0:T(8,128)(2,1)}), bf16[512,3584]{1,0:T(8,128)(2,1)}) %all-gather.6.cloned.1.call-update) | async-done | bytes 3670032 | tf_op jit(solution)/shard_map/all_gather | solution.py:115
  91.3 59.1 %all-gather.8.cloned.1.call-done = bf16[3584,1184]{0,1:T(8,128)(2,1)} async-done(((bf16[896,1184]{0,1:T(8,128)(2,1)}), bf16[3584,1184]{0,1:T(8,128)(2,1)}) %all-gather.8.cloned.1.call-update) | async-done | bytes 8486928 | tf_op jit(solution)/shard_map/all_gather | solution.py:118
  150.4 10.6 %fusion.27 = f32[512,1184]{0,1:T(8,128)} fusion(bf16[512,3584]{1,0:T(8,128)(2,1)} %all-gather.6.cloned.1.call-done, bf16[3584,1184]{0,1:T(8,128)(2,1)} %all-gather.8.cloned.1.call-done), kind=kOutput, calls=%fused_computation.48 | convolution fusion | flops 4345298944 | bytes 14581760 | tf_op jit(solution)/shard_map/dot_general | solution.py:116
  160.9 49.8 %all-gather.10.cloned.1.call-done = bf16[3584,1184]{0,1:T(8,128)(2,1)} async-done(((bf16[896,1184]{0,1:T(8,128)(2,1)}), bf16[3584,1184]{0,1:T(8,128)(2,1)}) %all-gather.10.cloned.1.call-update) | async-done | bytes 8486928 | tf_op jit(solution)/shard_map/all_gather | solution.py:123
  210.7 10.0 %fusion.2 = bf16[512,1184]{0,1:T(8,128)(2,1)S(1)} fusion(bf16[512,3584]{1,0:T(8,128)(2,1)} %all-gather.6.cloned.1.call-done, bf16[3584,1184]{0,1:T(8,128)(2,1)} %all-gather.10.cloned.1.call-done, f32[512,1184]{0,1:T(8,128)} %fusion.27), kind=kOutput, calls=%fused_computation.8 | convolution fusion | flops 4348936192 | bytes 15794176 | tf_op jit(solution)/shard_map/dot_general | solution.py:121
  220.8 50.2 %all-gather.12.cloned.1.call-done = bf16[1184,3584]{1,0:T(8,128)(2,1)} async-done(((bf16[1184,896]{1,0:T(8,128)(2,1)}), bf16[1184,3584]{1,0:T(8,128)(2,1)}) %all-gather.12.cloned.1.call-update) | async-done | bytes 8486928 | tf_op jit(solution)/shard_map/all_gather | solution.py:129
  270.9 9.8 %convolution_convert_fusion.1 = bf16[512,3584]{1,0:T(8,128)(2,1)} fusion(bf16[512,1184]{0,1:T(8,128)(2,1)S(1)} %fusion.2, bf16[1184,3584]{1,0:T(8,128)(2,1)} %all-gather.12.cloned.1.call-done), kind=kOutput, calls=%fused_computation.1 | convolution fusion | flops 4347133952 | bytes 13369344 | tf_op jit(solution)/shard_map/dot_general | solution.py:127
  280.8 0.6 copy-done.5
  281.9 0.6 copy.38
  282.5 3.2 all-to-all-start.1
  286.0 21.6 %psum.7 = f32[256]{0:T(256)S(1)} all-reduce(f32[256]{0:T(256)S(1)} %fusion.4), channel_id=1, replica_groups=mesh['group'=2,'dp'=2,'tensor'=8] {'tensor'}, use_global_device_ids=true, to_apply=%region_7.8 | all-reduce | flops 256 | bytes 2048 | tf_op jit(solution)/shard_map/psum | solution.py:95
  307.6 33.5 %reduce-scatter.8.cloned.1.call-done = bf16[32,3584]{1,0:T(8,128)(2,1)} async-done(((bf16[256,3584]{1,0:T(8,128)(2,1)}), bf16[32,3584]{1,0:T(8,128)(2,1)}) %reduce-scatter.8.cloned.1.call-update) | async-done | bytes 229392 | tf_op jit(solution)/shard_map/reduce_scatter | solution.py:98
  341.1 1.0 multiply_convert_fusion
  342.6 1.2 copy.40
  343.8 3.5 all-to-all-start.2
  347.5 7.9 %all-to-all-done.2 = bf16[2,32,3584]{2,0,1:T(2,128)(2,1)S(1)} async-done(((bf16[2,32,3584]{2,0,1:T(2,128)(2,1)}), bf16[2,32,3584]{2,0,1:T(2,128)(2,1)S(1)}, u32[]{:S(2)}, u32[]{:S(2)}) %all-to-all-start.2) | async-done | bytes 458784 | tf_op jit(solution)/shard_map/all_to_all | solution.py:40
  355.4 69.6 %reduce-scatter.6.cloned.1.call-done = bf16[64,3584]{1,0:T(8,128)(2,1)} async-done(((bf16[512,3584]{1,0:T(8,128)(2,1)}), bf16[64,3584]{1,0:T(8,128)(2,1)}) %reduce-scatter.6.cloned.1.call-update) | async-done | bytes 458768 | tf_op jit(solution)/shard_map/reduce_scatter | solution.py:132
  425.0 2.1 fusion.7
  427.3 66.6 %all-gather.14.cloned.1.call-done = bf16[512,3584]{1,0:T(8,128)(2,1)} async-done(((bf16[64,3584]{1,0:T(8,128)(2,1)}), bf16[512,3584]{1,0:T(8,128)(2,1)}) %all-gather.14.cloned.1.call-update) | async-done | bytes 3670032 | tf_op jit(solution)/shard_map/all_gather | solution.py:141
  493.8 8.7 %convolution_convert_fusion = bf16[3584,1184]{0,1:T(8,128)(2,1)} fusion(bf16[512,1184]{0,1:T(8,128)(2,1)S(1)} %fusion.2, bf16[512,3584]{1,0:T(8,128)(2,1)} %all-gather.14.cloned.1.call-done), kind=kOutput, calls=%fused_computation | convolution fusion | flops 4349542400 | bytes 13369344 | tf_op jit(solution)/shard_map/rc,rh->ch/dot_general | solution.py:143
  502.6 12.6 %copy.42 = bf16[3584,1184]{1,0:T(8,128)(2,1)} copy(bf16[3584,1184]{0,1:T(8,128)(2,1)} %convolution_convert_fusion) | data formatting | bytes 16973824
  515.2 75.1 %reduce-scatter.10.cloned.1.call-done = bf16[896,1184]{1,0:T(8,128)(2,1)} async-done(((bf16[3584,1184]{1,0:T(8,128)(2,1)}), bf16[896,1184]{1,0:T(8,128)(2,1)}) %reduce-scatter.10.cloned.1.call-update) | async-done | bytes 2121744
  590.3 3.2 copy.43
  593.5 2.3 convert_element_type.113
  (46 shorter events, 3.4 us)
Async XLA Ops:
  7.2 2.4 copy-start
  7.2 84.1 %all-gather.6.cloned.1.call-start = ((), (), s32[]{:S(2)}) async-start(), calls=%async_computation.6 | async-start | bytes 4128768 | tf_op jit(solution)/shard_map/all_gather | solution.py:115
  22.8 3.9 copy-start.2
  22.8 3.9 copy-start.4
  24.6 125.8 %all-gather.8.cloned.1.call-start = ((), (), s32[]{:S(2)}) async-start(), calls=%async_computation.7 | async-start | bytes 10608640 | tf_op jit(solution)/shard_map/all_gather | solution.py:118
  25.3 185.4 %all-gather.10.cloned.1.call-start = ((), (), s32[]{:S(2)}) async-start(), calls=%async_computation.8 | async-start | bytes 10608640 | tf_op jit(solution)/shard_map/all_gather | solution.py:123
  26.1 244.9 %all-gather.12.cloned.1.call-start = ((), (), s32[]{:S(2)}) async-start(), calls=%async_computation.9 | async-start | bytes 10608640 | tf_op jit(solution)/shard_map/all_gather | solution.py:129
  26.6 314.5 %reduce-scatter.8.cloned.1.call-start = ((), (), s32[]{:S(2)}) async-start(), calls=%async_computation.11 | async-start | bytes 2064384 | tf_op jit(solution)/shard_map/reduce_scatter | solution.py:98
  33.1 391.9 %reduce-scatter.6.cloned.1.call-start = ((), (), s32[]{:S(2)}) async-start(), calls=%async_computation.10 | async-start | bytes 4128768 | tf_op jit(solution)/shard_map/reduce_scatter | solution.py:132
  280.8 0.7 copy-start.5
  280.8 0.7 copy-start.3
  280.8 0.9 copy-start.6
  282.5 61.3 %all-to-all-start.1 = ((bf16[2,4,8]{2,0,1:T(2,128)(2,1)}), bf16[2,4,8]{2,0,1:T(2,128)(2,1)S(1)}, u32[]{:S(2)}, u32[]{:S(2)}) async-start(bf16[2,4,8]{2,0,1:T(2,128)(2,1)} %copy.38), calls=%async_computation.2 | async-start | bytes 4096 | tf_op jit(solution)/shard_map/all_to_all | solution.py:42
  343.8 11.6 %all-to-all-start.2 = ((bf16[2,32,3584]{2,0,1:T(2,128)(2,1)}), bf16[2,32,3584]{2,0,1:T(2,128)(2,1)S(1)}, u32[]{:S(2)}, u32[]{:S(2)}) async-start(bf16[2,32,3584]{2,0,1:T(2,128)(2,1)} %copy.40), calls=%async_computation.4 | async-start | bytes 917504 | tf_op jit(solution)/shard_map/all_to_all | solution.py:40
  347.3 146.5 %all-gather.14.cloned.1.call-start = ((), (), s32[]{:S(2)}) async-start(), calls=%async_computation.12 | async-start | bytes 4128768 | tf_op jit(solution)/shard_map/all_gather | solution.py:141
  427.2 163.1 %reduce-scatter.10.cloned.1.call-start = ((), (), s32[]{:S(2)}) async-start(), calls=%async_computation.13 | async-start | bytes 11468800
  590.3 5.5 copy-start.1
Sparse Core Ops, SparseCore 0:
  24.7 66.5 all-gather.5
  92.8 57.4 all-gather.7
  151.9 58.7 all-gather.9
  212.1 58.7 all-gather.11
  274.3 66.8 reduce-scatter.7
  345.2 79.7 reduce-scatter.5
  427.8 65.9 all-gather.13
  515.3 74.9 reduce-scatter.9
where the time goes:
time: 604 us; the launch traced here: 603 us
  waiting for transfers between devices  472 us (78%)
  matrix products  46.5 us (8%)
  blocking collectives  33.7 us (6%)
  local copies, waits for them, and re-layouts  19.2 us (3%)
  between operations  14.3 us (2%)
  other arithmetic  10.1 us (2%)
  starting transfers between devices  7.01 us (1%)
    unnamed x9, waiting for transfers between devices  77.1 us
    reduce_scatter x1, waiting for transfers between devices, local(): lax.psum_scatter(branch.astype(jnp.bfloat16), 'tensor', scatter_dimension...  69.6 us
    all_gather x1, waiting for transfers between devices, local(): grad_all = lax.all_gather(grad_block, 'tensor', axis=0, tiled=True)  66.6 us
    all_gather x1, waiting for transfers between devices, local(): lax.all_gather(gate_weight, ('group', 'dp'), axis=0, tiled=True)  59.1 us
    all_gather x1, waiting for transfers between devices, local(): gathered = lax.all_gather(normed, 'tensor', axis=0, tiled=True)  58.1 us
    all_gather x1, waiting for transfers between devices, local(): lax.all_gather(down_weight, ('group', 'dp'), axis=1, tiled=True)  50.2 us
    all_gather x1, waiting for transfers between devices, local(): lax.all_gather(up_weight, ('group', 'dp'), axis=0, tiled=True)  49.8 us
    reduce_scatter x1, waiting for transfers between devices, local(): lax.psum_scatter(jnp.dot(scaled, project_weight, preferred_element_type=j...  33.5 us
  transfers between devices with their start and end apart: 10, of which 9 were waited for; matrix products, arithmetic and copies ran while one was open for 7% of the time, Pallas kernels for 0%

commit v1 on v0

v1 whole, which is shorter than its diff:
```python
import math

import jax
import jax.numpy as jnp
from jax import lax
from jax.sharding import PartitionSpec as P

EP_LEN = 16
EXTRA = 128
EPSILON = 1e-06
OWNER_AXES = ("group", "dp")


def exchange(blocks):
    return lax.all_to_all(blocks, OWNER_AXES, split_axis=0, concat_axis=0, tiled=True)


def by_columns(rows, owners):
    return rows.reshape(rows.shape[0], owners, -1).transpose(1, 0, 2)


def three_terms(values):
    high = lax.reduce_precision(values, 8, 7)
    rest = values - high
    middle = lax.reduce_precision(rest, 8, 7)
    return high, middle, rest - middle


def build_selector(owner_list, owners, capacity):
    onehot = (owner_list[:, :, None] == jnp.arange(owners, dtype=jnp.int32)).astype(jnp.int32)
    earlier = jnp.cumsum(onehot, axis=1) - onehot
    rank_list = jnp.sum(earlier * onehot, axis=2)
    target = owner_list * capacity + rank_list
    slots = jnp.arange(owners * capacity, dtype=jnp.int32)
    return (target[:, None, :] == slots[None, :, None]).astype(jnp.bfloat16)


def local(
    teacher_hidden,
    teacher_gain,
    project_weight,
    student_hidden,
    student_gain,
    gate_weight,
    up_weight,
    down_weight,
    owner_map,
    token_ids,
    token_counts,
    id_weight,
):
    owners = lax.axis_size("group") * lax.axis_size("dp")
    tensors = lax.axis_size("tensor")
    tensor_index = lax.axis_index("tensor")
    owner_index = lax.axis_index(OWNER_AXES)
    episodes = token_counts.shape[0]
    own_span = EP_LEN // tensors
    share = own_span * episodes
    capacity = max(2, 2 * episodes // owners)
    received = owners * capacity
    student_width = student_hidden.shape[1]
    width = student_width // owners
    tokens_all = EP_LEN * episodes * owners
    teacher_width = teacher_hidden.shape[1] * tensors

    id_rows = token_ids.reshape(own_span, episodes)
    looked = jnp.sum(
        jnp.where(
            id_rows[:, :, None] == jnp.arange(id_weight.shape[0], dtype=jnp.int32)[None, None, :],
            id_weight[None, None, :],
            0.0,
        ),
        axis=2,
    )
    position = tensor_index * own_span + jnp.arange(own_span, dtype=jnp.int32)[:, None]
    token_weight = jnp.where(position < token_counts[None, :], looked, 0.0).reshape(share, 1)

    own_rows = student_hidden.astype(jnp.float32)
    own_rescale = lax.rsqrt(jnp.mean(own_rows * own_rows, axis=1, keepdims=True) + EPSILON)
    owner_rows = jnp.tile(owner_map.astype(jnp.float32), (own_span, 1))
    extras = jnp.concatenate([token_weight, owner_rows, *three_terms(own_rescale)], axis=1)
    extras = jnp.pad(extras, ((0, 0), (0, EXTRA - extras.shape[1]))).astype(jnp.bfloat16)
    arrived = exchange(
        jnp.concatenate(
            [
                by_columns(student_hidden, owners),
                jnp.broadcast_to(extras[None], (owners, share, EXTRA)),
            ],
            axis=2,
        )
    )
    rows = owners * share
    student_block = arrived[:, :, :width].reshape(rows, width).astype(jnp.float32)
    facts = arrived[:, :, width:].astype(jnp.float32)
    weight_rows = facts[:, :, 0].reshape(rows, 1)
    owner_list = facts[:, :episodes, 1].astype(jnp.int32)
    rescale = (facts[:, :, 2] + facts[:, :, 3] + facts[:, :, 4]).reshape(rows, 1)
    gain = lax.dynamic_slice_in_dim(student_gain, owner_index * width, width, 0)
    normed = (student_block * rescale * gain[None, :]).astype(jnp.bfloat16)
    gathered = lax.all_gather(normed, "tensor", axis=0, tiled=True)

    widened = teacher_hidden.astype(jnp.float32)
    squares = jnp.sum(widened * widened, axis=1)
    scaled = (widened * teacher_gain[None, :]).astype(jnp.bfloat16)
    inverse = lax.rsqrt(lax.psum(squares, "tensor") / teacher_width + EPSILON)
    summed = lax.psum_scatter(
        jnp.dot(scaled, project_weight, preferred_element_type=jnp.float32).astype(jnp.bfloat16),
        "tensor",
        scatter_dimension=0,
        tiled=True,
    ).astype(jnp.float32)
    own_inverse = lax.dynamic_slice_in_dim(inverse, tensor_index * share, share, 0)
    projected = exchange(by_columns((summed * own_inverse[:, None]).astype(jnp.bfloat16), owners))

    hidden = gate_weight.shape[1]
    gate_part = jnp.dot(gathered, gate_weight, preferred_element_type=jnp.float32)
    up_part = jnp.dot(gathered, up_weight, preferred_element_type=jnp.float32)
    parts = jnp.stack(
        [
            gate_part.astype(jnp.bfloat16).reshape(owners, -1, hidden),
            up_part.astype(jnp.bfloat16).reshape(owners, -1, hidden),
        ],
        axis=1,
    )
    sums = lax.psum_scatter(parts, OWNER_AXES, scatter_dimension=0, tiled=True).astype(jnp.float32)
    activated = (jax.nn.silu(sums[0, 0]) * sums[0, 1]).astype(jnp.bfloat16)
    act_all = lax.all_gather(activated, OWNER_AXES, axis=0, tiled=True)
    branch = jnp.dot(act_all, down_weight, preferred_element_type=jnp.float32)
    branch_local = lax.psum_scatter(
        branch.astype(jnp.bfloat16), "tensor", scatter_dimension=0, tiled=True
    ).astype(jnp.float32)
    predicted = student_block + branch_local

    difference = predicted - projected.reshape(rows, width).astype(jnp.float32)
    grad_block = (weight_rows * difference * (1.0 / math.sqrt(tokens_all))).astype(jnp.bfloat16)
    grad_all = lax.all_gather(grad_block, "tensor", axis=0, tiled=True)
    down_grad = jnp.einsum("rc,rh->ch", grad_all, act_all, preferred_element_type=jnp.float32)

    selector = build_selector(owner_list, owners, capacity)
    picked = jnp.einsum(
        "sre,spef->sprf",
        selector,
        predicted.astype(jnp.bfloat16).reshape(owners, own_span, episodes, width),
        preferred_element_type=jnp.float32,
    ).astype(jnp.bfloat16)
    outgoing = picked.reshape(owners, own_span, owners, capacity, width).transpose(2, 1, 0, 3, 4)
    incoming = exchange(outgoing.reshape(owners, own_span, received, width))
    student_out = incoming.transpose(1, 2, 0, 3).reshape(1, own_span, received, student_width)
    return (student_out, down_grad)


def solution(mesh):
    in_specs = (
        P(("group", "dp"), "tensor"),
        P("tensor"),
        P("tensor", None),
        P(("group", "dp", "tensor"), None),
        P(),
        P(("group", "dp"), "tensor"),
        P(("group", "dp"), "tensor"),
        P("tensor", ("group", "dp")),
        P(("group", "dp"), None),
        P(("group", "dp", "tensor")),
        P(("group", "dp")),
        P(),
    )
    out_specs = (P(("group", "dp"), "tensor", None, None), P(("group", "dp"), "tensor"))
    return jax.shard_map(local, mesh=mesh, in_specs=in_specs, out_specs=out_specs, check_vma=False)
```

time: 604 us -> 379 us (0.63)
  waiting for transfers between devices: 472 us -> 258 us
  matrix products: 46.5 us -> 29.6 us
    all_gather x3 -> x1, waiting for transfers between devices: 159 us -> 18.4 us  [local(): act_all = lax.all_gather(activated, OWNER_AXES, axis=0, tiled=True)]
    unnamed x9 -> x6, waiting for transfers between devices: 77.1 us -> 0.1 us
    reduce_scatter x0 -> x1, waiting for transfers between devices: none -> 47.6 us  [local(): lax.psum_scatter(parts, OWNER_AXES, scatter_dimension=0, tiled=True)]
    all_gather x1, waiting for transfers between devices: 66.6 us -> 33.1 us  [local(): grad_all = lax.all_gather(grad_block, 'tensor', axis=0, tiled=True)]
    another operation x0 -> x6, local copies, waits for them, and re-layouts: none -> 17.3 us  [the longest x4 17.2 us: local(): jnp.stack([gate_part.astype(jnp.bfloat16).reshape(owners, -1, hidden), up...]
    dot_general x7 -> x5, matrix products: 40.1 us -> 23.2 us  [the longest x1 6.93 us: local(): jnp.einsum('rc,rh->ch', grad_all, act_all, preferred_element_type=jnp.flo...]
    unnamed x16 -> x13, local copies, waits for them, and re-layouts: 16.4 us -> 0.39 us
    reduce_scatter x1, waiting for transfers between devices: 69.6 us -> 58.9 us  [local(): lax.psum_scatter(branch.astype(jnp.bfloat16), 'tensor', scatter_dimension...]
  transfers between devices with their start and end apart: 10 -> 8, of which waited for: 9 -> 8; matrix products, arithmetic and copies ran while one was open for 7% -> 5% of each run, Pallas kernels for 0% -> 0%
where the time goes in v1:
time: 379 us
  waiting for transfers between devices  258 us (68%)
  blocking collectives  32 us (8%)
  matrix products  29.6 us (8%)
  local copies, waits for them, and re-layouts  22.6 us (6%)
  between operations  14.3 us (4%)
  other arithmetic  14.1 us (4%)
  starting transfers between devices  8.01 us (2%)
    reduce_scatter x1, waiting for transfers between devices, local(): lax.psum_scatter(branch.astype(jnp.bfloat16), 'tensor', scatter_dimension...  58.9 us
    reduce_scatter x1, waiting for transfers between devices, local(): lax.psum_scatter(parts, OWNER_AXES, scatter_dimension=0, tiled=True)  47.6 us
    all_gather x1, waiting for transfers between devices, local(): gathered = lax.all_gather(normed, 'tensor', axis=0, tiled=True)  47.4 us
    reduce_scatter x1, waiting for transfers between devices, local(): lax.psum_scatter(jnp.dot(scaled, project_weight, preferred_element_type=j...  41.9 us
    all_gather x1, waiting for transfers between devices, local(): grad_all = lax.all_gather(grad_block, 'tensor', axis=0, tiled=True)  33.1 us
    psum x1, blocking collectives, local(): inverse = lax.rsqrt(lax.psum(squares, 'tensor') / teacher_width + EPSILON)  21.4 us
    all_gather x1, waiting for transfers between devices, local(): act_all = lax.all_gather(activated, OWNER_AXES, axis=0, tiled=True)  18.4 us
    another operation x4, local copies, waits for them, and re-layouts, local(): jnp.stack([gate_part.astype(jnp.bfloat16).reshape(owners, -1, hidden), up...  17.2 us
  transfers between devices with their start and end apart: 8, of which 8 were waited for; matrix products, arithmetic and copies ran while one was open for 5% of the time, Pallas kernels for 0%

profile of v1, /device:TPU:0, one launch (start us, length us, event | category | flops | bytes accessed | tf_op | source)
XLA Modules:
  0.0 378.6 jit_solution(4953372782439392148)
XLA Ops:
  7.2 1.2 multiply_reduce_fusion
  8.4 1.0 reshape.158
  10.2 0.8 select_reduce_fusion
  13.5 4.2 %all-to-all-start = ((bf16[4,32,1024]{2,1,0:T(8,128)(2,1)}), bf16[4,32,1024]{2,1,0:T(8,128)(2,1)S(1)}, u32[]{:S(2)}, u32[]{:S(2)}) async-start(bf16[4,32,1024]{2,1,0:T(8,128)(2,1)} %pad_maximum_fusion.1), calls=%async_computation | async-start | bytes 524288 | tf_op jit(solution)/shard_map/all_to_all | solution.py:15
  17.8 0.8 dynamic_slice.6
  18.6 5.2 %all-to-all-done = bf16[4,32,1024]{2,1,0:T(8,128)(2,1)S(1)} async-done(((bf16[4,32,1024]{2,1,0:T(8,128)(2,1)}), bf16[4,32,1024]{2,1,0:T(8,128)(2,1)S(1)}, u32[]{:S(2)}, u32[]{:S(2)}) %all-to-all-start) | async-done | bytes 262176 | tf_op jit(solution)/shard_map/all_to_all | solution.py:15
  24.1 0.8 fusion.8
  25.0 47.4 %all-gather.4.cloned.1.call-done = bf16[1024,896]{1,0:T(8,128)(2,1)} async-done(((bf16[128,896]{1,0:T(8,128)(2,1)}), bf16[1024,896]{1,0:T(8,128)(2,1)}) %all-gather.4.cloned.1.call-update) | async-done | bytes 1835024 | tf_op jit(solution)/shard_map/all_gather | solution.py:100
  72.4 5.5 %convolution_convert_fusion.2 = bf16[1024,1184]{0,1:T(8,128)(2,1)} fusion(bf16[1024,896]{1,0:T(8,128)(2,1)} %all-gather.4.cloned.1.call-done, bf16[896,1184]{0,1:T(8,128)(2,1)S(1)} %copy-done), kind=kOutput, calls=%fused_computation.3 | convolution fusion | flops 2173861888 | bytes 6381568 | tf_op jit(solution)/shard_map/dot_general | solution.py:116
  77.9 5.7 %stack_reshape.6 = bf16[4,1,256,1184]{2,0,3,1:T(4,128)(2,1)} reshape(bf16[1024,1184]{0,1:T(8,128)(2,1)} %convolution_convert_fusion.2) | data formatting | bytes 4849664 | tf_op jit(solution)/shard_map/stack;reshape | solution.py:118
  83.6 3.6 copy.44
  87.2 4.0 %convolution_convert_fusion.1 = bf16[1024,1184]{0,1:T(8,128)(2,1)} fusion(bf16[1024,896]{1,0:T(8,128)(2,1)S(1)} %copy-done.4, bf16[896,1184]{0,1:T(8,128)(2,1)S(1)} %copy-done.3), kind=kOutput, calls=%fused_computation.2 | convolution fusion | flops 2173861888 | bytes 6381568 | tf_op jit(solution)/shard_map/dot_general | solution.py:117
  91.2 5.7 %stack_reshape.7 = bf16[4,1,256,1184]{2,0,3,1:T(4,128)(2,1)} reshape(bf16[1024,1184]{0,1:T(8,128)(2,1)} %convolution_convert_fusion.1) | data formatting | bytes 4849664 | tf_op jit(solution)/shard_map/stack;reshape | solution.py:118
  96.9 2.1 copy.45
  99.3 2.6 pad_maximum_fusion
  102.0 47.6 %reduce-scatter.4.cloned.1.call-done = bf16[1,2,256,1184]{2,3,1,0:T(8,128)(2,1)} async-done(((bf16[4,2,256,1184]{2,3,1,0:T(8,128)(2,1)}), bf16[1,2,256,1184]{2,3,1,0:T(8,128)(2,1)}) %reduce-scatter.4.cloned.1.call-update) | async-done | bytes 1212432 | tf_op jit(solution)/shard_map/reduce_scatter | solution.py:125
  149.6 1.4 convert_element_type.93
  151.1 1.2 fusion.2
  152.3 6.4 %convolution_convert_fusion = bf16[256,3584]{1,0:T(8,128)(2,1)} fusion(bf16[1024,3584]{1,0:T(8,128)(2,1)} %param.14, bf16[256,1024]{1,0:T(8,128)(2,1)S(1)} %copy-done.2, f32[1024]{0:T(1024)S(1)} %copy-done.5), kind=kOutput, calls=%fused_computation | convolution fusion | flops 1880752128 | bytes 9703424 | tf_op jit(solution)/shard_map/dot_general | solution.py:107
  158.8 18.4 %all-gather.6.cloned.1.call-done = bf16[1024,1184]{0,1:T(8,128)(2,1)} async-done(((bf16[256,1184]{0,1:T(8,128)(2,1)}), bf16[1024,1184]{0,1:T(8,128)(2,1)}) %all-gather.6.cloned.1.call-update) | async-done | bytes 2424848 | tf_op jit(solution)/shard_map/all_gather | solution.py:127
  177.1 6.5 %convolution_convert_fusion.3 = bf16[1024,896]{1,0:T(8,128)(2,1)} fusion(bf16[1024,1184]{0,1:T(8,128)(2,1)} %all-gather.6.cloned.1.call-done, bf16[1184,896]{1,0:T(8,128)(2,1)} %param.19), kind=kOutput, calls=%fused_computation.4 | convolution fusion | flops 2173566976 | bytes 6381568 | tf_op jit(solution)/shard_map/dot_general | solution.py:128
  183.8 21.4 %psum.7 = f32[256]{0:T(256)S(1)} all-reduce(f32[256]{0:T(256)S(1)} %fusion.4), channel_id=1, replica_groups=mesh['group'=2,'dp'=2,'tensor'=8] {'tensor'}, use_global_device_ids=true, to_apply=%region_8.9 | all-reduce | flops 256 | bytes 2048 | tf_op jit(solution)/shard_map/psum | solution.py:105
  205.3 41.9 %reduce-scatter.8.cloned.1.call-done = bf16[32,3584]{1,0:T(8,128)(2,1)} async-done(((bf16[256,3584]{1,0:T(8,128)(2,1)}), bf16[32,3584]{1,0:T(8,128)(2,1)}) %reduce-scatter.8.cloned.1.call-update) | async-done | bytes 229392 | tf_op jit(solution)/shard_map/reduce_scatter | solution.py:106
  247.2 1.0 multiply_convert_fusion
  249.0 3.4 all-to-all-start.2
  252.7 5.3 %all-to-all-done.2 = bf16[4,32,896]{2,1,0:T(8,128)(2,1)S(1)} async-done(((bf16[4,32,896]{2,1,0:T(8,128)(2,1)}), bf16[4,32,896]{2,1,0:T(8,128)(2,1)S(1)}, u32[]{:S(2)}, u32[]{:S(2)}) %all-to-all-start.2) | async-done | bytes 229408 | tf_op jit(solution)/shard_map/all_to_all | solution.py:15
  258.0 58.9 %reduce-scatter.6.cloned.1.call-done = bf16[128,896]{1,0:T(8,128)(2,1)} async-done(((bf16[1024,896]{1,0:T(8,128)(2,1)}), bf16[128,896]{1,0:T(8,128)(2,1)}) %reduce-scatter.6.cloned.1.call-update) | async-done | bytes 229392 | tf_op jit(solution)/shard_map/reduce_scatter | solution.py:129
  316.8 1.8 fusion.11
  319.7 10.6 %all_to_all.15 = bf16[4,2,32,896]{3,2,1,0:T(8,128)(2,1)S(1)} all-to-all(bf16[4,2,32,896]{3,2,1,0:T(8,128)(2,1)S(1)} %bitcast.65), channel_id=1, replica_groups=mesh['group'=2,'dp'=2,'tensor'=8] {'group','dp'}, dimensions={0} | all-to-all | bytes 917504 | tf_op jit(solution)/shard_map/all_to_all | solution.py:15
  330.7 0.9 reshape.162
  331.6 33.1 %all-gather.8.cloned.1.call-done = bf16[1024,896]{1,0:T(8,128)(2,1)} async-done(((bf16[128,896]{1,0:T(8,128)(2,1)}), bf16[1024,896]{1,0:T(8,128)(2,1)}) %all-gather.8.cloned.1.call-update) | async-done | bytes 1835024 | tf_op jit(solution)/shard_map/all_gather | solution.py:136
  364.8 6.9 %fusion.21 = f32[896,1184]{0,1:T(8,128)} fusion(bf16[1024,1184]{0,1:T(8,128)(2,1)} %all-gather.6.cloned.1.call-done, bf16[1024,896]{1,0:T(8,128)(2,1)} %all-gather.8.cloned.1.call-done), kind=kOutput, calls=%fused_computation.57 | convolution fusion | flops 2172649472 | bytes 8503296 | tf_op jit(solution)/shard_map/rc,rh->ch/dot_general | solution.py:137
  (55 shorter events, 6.8 us)
Async XLA Ops:
  7.2 65.3 %copy-start = (bf16[896,1184]{0,1:T(8,128)(2,1)S(1)}, bf16[896,1184]{0,1:T(8,128)(2,1)}, u32[]{:S(2)}) copy-start(bf16[896,1184]{0,1:T(8,128)(2,1)} %param.17) | copy-start | bytes 6365188
  13.5 10.2 %all-to-all-start = ((bf16[4,32,1024]{2,1,0:T(8,128)(2,1)}), bf16[4,32,1024]{2,1,0:T(8,128)(2,1)S(1)}, u32[]{:S(2)}, u32[]{:S(2)}) async-start(bf16[4,32,1024]{2,1,0:T(8,128)(2,1)} %pad_maximum_fusion.1), calls=%async_computation | async-start | bytes 524288 | tf_op jit(solution)/shard_map/all_to_all | solution.py:15
  17.8 54.7 %all-gather.4.cloned.1.call-start = ((), (), s32[]{:S(2)}) async-start(), calls=%async_computation.6 | async-start | bytes 2064384 | tf_op jit(solution)/shard_map/all_gather | solution.py:100
  25.0 124.6 %reduce-scatter.4.cloned.1.call-start = ((), (), s32[]{:S(2)}) async-start(), calls=%async_computation.7 | async-start | bytes 6062080 | tf_op jit(solution)/shard_map/reduce_scatter | solution.py:125
  83.6 3.6 copy-start.3
  83.6 3.6 copy-start.4
  96.9 2.4 copy-start.1
  101.9 75.2 %all-gather.6.cloned.1.call-start = ((), (), s32[]{:S(2)}) async-start(), calls=%async_computation.8 | async-start | bytes 3031040 | tf_op jit(solution)/shard_map/all_gather | solution.py:127
  151.0 1.3 copy-start.2
  151.1 1.3 copy-start.5
  152.3 94.9 %reduce-scatter.8.cloned.1.call-start = ((), (), s32[]{:S(2)}) async-start(), calls=%async_computation.10 | async-start | bytes 2064384 | tf_op jit(solution)/shard_map/reduce_scatter | solution.py:106
  158.7 158.1 %reduce-scatter.6.cloned.1.call-start = ((), (), s32[]{:S(2)}) async-start(), calls=%async_computation.9 | async-start | bytes 2064384 | tf_op jit(solution)/shard_map/reduce_scatter | solution.py:129
  249.0 9.0 %all-to-all-start.2 = ((bf16[4,32,896]{2,1,0:T(8,128)(2,1)}), bf16[4,32,896]{2,1,0:T(8,128)(2,1)S(1)}, u32[]{:S(2)}, u32[]{:S(2)}) async-start(bf16[4,32,896]{2,1,0:T(8,128)(2,1)} %bitcast.64), calls=%async_computation.5 | async-start | bytes 458752 | tf_op jit(solution)/shard_map/all_to_all | solution.py:15
  252.4 112.4 %all-gather.8.cloned.1.call-start = ((), (), s32[]{:S(2)}) async-start(), calls=%async_computation.11 | async-start | bytes 2064384 | tf_op jit(solution)/shard_map/all_gather | solution.py:136
Sparse Core Ops, SparseCore 0:
  25.1 47.3 all-gather.3
  102.0 47.4 reduce-scatter.3
  152.4 24.7 all-gather.5
  180.5 66.7 reduce-scatter.7
  251.1 65.6 reduce-scatter.5
  319.5 45.2 all-gather.7
